TPU v7x, 512 devices: a whole 4x4x16 slice. The times are simulated.
512 devices in a mesh: section: 4 (over x), seq: 16 (over y, z_lo), wide: 8 (over z_hi, core).
Axes of the slice: x: 4, y: 4, z: 16 (z_hi: 4, z_lo: 4; z = z_hi * 4 + z_lo), core: 2. Of those that a mesh axis runs over, the one named last changes fastest.
Arguments:
- q_self: bfloat16 [4, 4096, 5120], P('section', 'seq', 'wide'), may hold values from -6 to 6
- k_self: bfloat16 [4, 4096, 5120], P('section', 'seq', 'wide'), may hold values from -6 to 6
- v_self: bfloat16 [4, 4096, 5120], P('section', 'seq', 'wide'), may hold values from -6 to 6
- gain_q_self: float32 [5120], P('wide'), may hold values from 1.2 to 2.4
- gain_k_self: float32 [5120], P('wide'), may hold values from 1.2 to 2.4
- counts: int32 [4], replicated, may hold values from 1 to 4096, 12288 in all
- q_cross: bfloat16 [4, 4096, 5120], P('section', 'seq', 'wide'), may hold values from -6 to 6
- cap_kv: bfloat16 [2, 4, 512, 5120], P(None, 'section', 'seq', 'wide'), may hold values from -6 to 6
- gain_q_cross: float32 [5120], P('wide'), may hold values from 1.2 to 2.4
- gain_k_cross: float32 [5120], P('wide'), may hold values from 1.2 to 2.4
- cap_len: int32 [4], replicated, may hold values from 1 to 512, 1024 in all
- owner: int32 [4], replicated, may hold values from 0 to 3, each once
Outputs:
- out_self: bfloat16 [4, 4096, 5120], P('section', 'seq', 'wide')
- out_cross: bfloat16 [4, 4096, 5120], P('section', 'seq', 'wide')
Inputs may be any that keep to these rules, and one draw needn't show every extreme that they name: owner is a permutation of the clips.
All inputs are finite; a program needn't handle non-finite values.
Results may differ from a plain program's by a relative error of at most 0.012.
The roundings to bfloat16 on the way count: a program that leaves them out, or rounds other values in their place, can miss the bound.
Values may be sent and summed in bfloat16 or wider, within the bound.
A program may use at most 128 MiB of HBM per device.

v0:
```python
import math
import jax
import jax.numpy as jnp
from jax import lax
from jax.sharding import PartitionSpec as P

D = 5120
HEAD = 128
masked_score = -1e30


def square_sums(values):
    floats = values.astype(jnp.float32)
    return jnp.sum(floats * floats, axis=-1)


def scaled_rows(values, total_squares, gain):
    floats = values.astype(jnp.float32)
    factor = lax.rsqrt(total_squares / D + 1e-06)
    return (floats * factor[:, None] * gain[None, :]).astype(jnp.bfloat16)


def start_state(heads_here, rows):
    running = jnp.full((heads_here, rows), masked_score, jnp.float32)
    totals = jnp.zeros((heads_here, rows), jnp.float32)
    accum = jnp.zeros((heads_here, rows, HEAD), jnp.float32)
    return (running, totals, accum)


def attend_rows(state, queries, keys, values, limit):
    heads_here = queries.shape[1]
    count_rows = keys.shape[0]
    block_rows = math.gcd(count_rows, 512)
    blocks = count_rows // block_rows
    key_blocks = keys.reshape(blocks, block_rows, heads_here, HEAD)
    value_blocks = values.reshape(blocks, block_rows, heads_here, HEAD)
    factor = 1.0 / math.sqrt(HEAD)

    def one_block(carry, inputs):
        running, totals, accum = carry
        key_block, value_block, number = inputs
        scores = (
            jnp.einsum("qhd,khd->hqk", queries, key_block, preferred_element_type=jnp.float32)
            * factor
        )
        position = number * block_rows + jnp.arange(block_rows, dtype=jnp.int32)
        scores = jnp.where((position < limit)[None, None, :], scores, masked_score)
        newest = jnp.maximum(running, jnp.max(scores, axis=-1))
        rescale = jnp.exp(running - newest)
        weights = jnp.exp(scores - newest[:, :, None])
        totals = totals * rescale + jnp.sum(weights, axis=-1)
        update = jnp.einsum(
            "hqk,khd->hqd",
            weights.astype(jnp.bfloat16),
            value_block,
            preferred_element_type=jnp.float32,
        )
        accum = accum * rescale[:, :, None] + update
        return ((newest, totals, accum), None)

    numbers = jnp.arange(blocks, dtype=jnp.int32)
    state, unused = lax.scan(one_block, state, (key_blocks, value_blocks, numbers))
    return state


def finish(state):
    running, totals, accum = state
    result = accum / totals[:, :, None]
    heads_here, rows, width = result.shape
    return result.transpose(1, 0, 2).reshape(rows, heads_here * width).astype(jnp.bfloat16)[None]


def per_device(
    q_self,
    k_self,
    v_self,
    gain_q_self,
    gain_k_self,
    counts,
    q_cross,
    cap_kv,
    gain_q_cross,
    gain_k_cross,
    cap_len,
    owner,
):
    rows = q_self.shape[1]
    heads_here = q_self.shape[2] // HEAD
    section_index = lax.axis_index("section")
    section_count = lax.axis_size("section")
    latent_count = lax.dynamic_index_in_dim(counts, section_index, 0, keepdims=False)
    totals = lax.psum(
        (square_sums(q_self[0]), square_sums(k_self[0]), square_sums(q_cross[0])), "wide"
    )
    q_hat = scaled_rows(q_self[0], totals[0], gain_q_self).reshape(rows, heads_here, HEAD)
    k_hat = scaled_rows(k_self[0], totals[1], gain_k_self)
    cross_hat = scaled_rows(q_cross[0], totals[2], gain_q_cross).reshape(rows, heads_here, HEAD)
    keys = lax.all_gather(k_hat[None], "seq", axis=1, tiled=True)
    values = lax.all_gather(v_self, "seq", axis=1, tiled=True)
    count_rows = keys.shape[1]
    self_state = attend_rows(
        start_state(heads_here, rows),
        q_hat,
        keys[0].reshape(count_rows, heads_here, HEAD),
        values[0].reshape(count_rows, heads_here, HEAD),
        latent_count,
    )
    out_self = finish(self_state)
    section_numbers = jnp.arange(section_count, dtype=jnp.int32)
    source = jnp.sum(jnp.where(owner == section_index, section_numbers, 0))
    caption_length = lax.dynamic_index_in_dim(cap_len, source, 0, keepdims=False)
    whole = lax.all_gather(cap_kv, "seq", axis=2, tiled=True)
    key_totals = lax.psum(square_sums(whole[0, 0]), "wide")
    own_keys = scaled_rows(whole[0, 0], key_totals, gain_k_cross)
    assembled = jnp.stack([own_keys, whole[1, 0]])[:, None]
    routed = lax.all_gather(assembled, "section", axis=1, tiled=True)
    chosen = lax.dynamic_index_in_dim(routed, source, 1, keepdims=False)
    count_rows = chosen.shape[1]
    cross_state = attend_rows(
        start_state(heads_here, rows),
        cross_hat,
        chosen[0].reshape(count_rows, heads_here, HEAD),
        chosen[1].reshape(count_rows, heads_here, HEAD),
        caption_length,
    )
    out_cross = finish(cross_state)
    return (out_self, out_cross)


def solution(mesh):
    return jax.shard_map(
        per_device,
        mesh=mesh,
        in_specs=(
            P("section", "seq", "wide"),
            P("section", "seq", "wide"),
            P("section", "seq", "wide"),
            P("wide"),
            P("wide"),
            P(),
            P("section", "seq", "wide"),
            P(None, "section", "seq", "wide"),
            P("wide"),
            P("wide"),
            P(),
            P(),
        ),
        out_specs=(P("section", "seq", "wide"), P("section", "seq", "wide")),
        check_vma=False,
    )
```

profile of v0, /device:TPU:1, one launch (start us, length us, event | category | flops | bytes accessed | tf_op | source)
XLA Modules:
  0.0 517.4 jit_solution(16021521661886454871)
XLA Ops:
  7.2 0.7 all-gather.10.cloned.1.call-update
  8.0 0.7 all-gather.8.cloned.1.call-update
  8.7 1.1 copy.40
  9.8 1.1 copy.34
  11.2 1.1 fusion.47
  12.3 82.7 %all-gather.10.cloned.1.call-done = bf16[2,1,512,640]{3,2,1,0:T(8,128)(2,1)} async-done(((bf16[2,1,32,640]{3,2,1,0:T(8,128)(2,1)}), bf16[2,1,512,640]{3,2,1,0:T(8,128)(2,1)}) %all-gather.10.cloned.1.call-update) | async-done | bytes 1310736 | tf_op jit(solution)/shard_map/all_gather | solution.py:112
  95.1 1.3 fusion.28
  96.4 27.6 %all-reduce = (f32[256]{0:T(256)S(1)}, f32[256]{0:T(256)S(1)}, f32[512]{0:T(512)S(1)}, f32[256]{0:T(256)S(1)}) all-reduce(f32[256]{0:T(256)S(1)} %fusion.47, f32[256]{0:T(256)S(1)} %multiply_reduce_fusion.1, f32[512]{0:T(512)S(1)} %fusion.28, f32[256]{0:T(256)S(1)} %multiply_reduce_fusion), channel_id=1, replica_groups=mesh['section'=4,'seq'=16,'wide'=8] {'wide'}, use_global_device_ids=true, to_apply=%region_1.2 | all-reduce | flops 1280 | bytes 10240 | tf_op jit(solution)/shard_map/psum | solution.py:92
  124.0 1.1 slice_bitcast_fusion
  125.2 1.4 fusion.27
  126.6 1.3 pad_maximum_fusion
  128.0 0.9 fusion.49
  128.9 0.6 fusion.53
  131.5 0.6 dynamic_slice.31
  132.6 0.6 iota_compare_fusion
  133.7 98.9 %all-gather.8.cloned.1.call-done = bf16[1,4096,640]{2,1,0:T(8,128)(2,1)} async-done(((bf16[1,256,640]{2,1,0:T(8,128)(2,1)}), bf16[1,4096,640]{2,1,0:T(8,128)(2,1)}) %all-gather.8.cloned.1.call-update) | async-done | bytes 5242896 | tf_op jit(solution)/shard_map/all_gather | solution.py:99
  232.6 12.6 %reshape.180 = bf16[8,512,5,128]{3,2,1,0:T(8,128)(2,1)} reshape(bf16[1,4096,640]{2,1,0:T(8,128)(2,1)} %all-gather.8.cloned.1.call-done) | data formatting | bytes 10485760 | tf_op jit(solution)/shard_map/reshape;reshape;squeeze | solution.py:36
  245.3 7.2 %copy.38 = bf16[8,512,5,128]{3,1,2,0:T(8,128)(2,1)} copy(bf16[8,512,5,128]{3,2,1,0:T(8,128)(2,1)} %reshape.180) | data formatting | bytes 10485760
  252.5 44.5 %all-gather.12.cloned.1.call-done = bf16[2,2048,640]{2,1,0:T(8,128)(2,1)} async-done(((bf16[2,512,640]{2,1,0:T(8,128)(2,1)}), bf16[2,2048,640]{2,1,0:T(8,128)(2,1)}) %all-gather.12.cloned.1.call-update) | async-done | bytes 5242896 | tf_op jit(solution)/shard_map/all_gather | solution.py:116
  297.0 1.4 constant_dynamic-slice_fusion
  299.0 1.0 fusion.22
  300.0 0.8 fusion.23
  300.7 0.8 fusion.44
  301.6 0.9 copy.46
  302.5 125.5 %all-gather.6.cloned.1.call-done = bf16[1,4096,640]{2,1,0:T(8,128)(2,1)} async-done(((bf16[1,256,640]{2,1,0:T(8,128)(2,1)}), bf16[1,4096,640]{2,1,0:T(8,128)(2,1)}) %all-gather.6.cloned.1.call-update) | async-done | bytes 5242896 | tf_op jit(solution)/shard_map/all_gather | solution.py:98
  428.0 12.6 %reshape.179 = bf16[8,512,5,128]{3,2,1,0:T(8,128)(2,1)} reshape(bf16[1,4096,640]{2,1,0:T(8,128)(2,1)} %all-gather.6.cloned.1.call-done) | data formatting | bytes 10485760 | tf_op jit(solution)/shard_map/reshape;reshape;squeeze | solution.py:35
  440.6 7.1 %copy.36 = bf16[8,512,5,128]{3,1,2,0:T(8,128)(2,1)} copy(bf16[8,512,5,128]{3,2,1,0:T(8,128)(2,1)} %reshape.179) | data formatting | bytes 10485760
  447.8 60.8 %while.3 = (s32[]{:T(128)}, f32[5,256]{1,0:T(8,128)S(1)}, f32[5,256]{1,0:T(8,128)S(1)}, f32[5,256,128]{2,1,0:T(8,128)}, s32[8]{0:T(128)S(1)}, /*index=5*/s32[]{:...) while((s32[]{:T(128)}, f32[5,256]{1,0:T(8,128)S(1)}, ...), condition=%wide.region_7.8_spmd.clone, body=%wide.region_4.7_spmd.clone.sunk | while | flops 343252224 | bytes 16141529 | solution.py:62
  447.8 0.6 dynamic_slice.51
  449.5 1.6 bitcast_reduce_fusion.2
  451.2 0.6 fusion.69
  452.3 2.1 fusion.71
  454.5 0.9 copy-done.2
  457.1 1.6 bitcast_reduce_fusion.2
  458.8 0.6 fusion.69
  459.9 2.1 fusion.71
  462.1 0.9 copy-done.2
  464.8 1.6 bitcast_reduce_fusion.2
  466.4 0.6 fusion.69
  467.5 2.1 fusion.71
  469.7 0.9 copy-done.2
  472.4 1.6 bitcast_reduce_fusion.2
  474.0 0.6 fusion.69
  475.1 2.1 fusion.71
  477.3 0.9 copy-done.2
  478.2 0.6 dynamic_slice.51
  480.0 1.6 bitcast_reduce_fusion.2
  481.6 0.6 fusion.69
  482.7 2.1 fusion.71
  484.9 0.9 copy-done.2
  487.6 1.6 bitcast_reduce_fusion.2
  489.2 0.6 fusion.69
  490.3 2.1 fusion.71
  492.5 0.9 copy-done.2
  495.2 1.6 bitcast_reduce_fusion.2
  496.9 0.6 fusion.69
  497.9 2.1 fusion.71
  500.1 0.9 copy-done.2
  502.8 1.6 bitcast_reduce_fusion.2
  504.5 0.6 fusion.69
  505.5 2.1 fusion.71
  507.7 0.9 copy-done.2
  508.6 1.3 copy.39
  510.0 0.9 copy.45
  (101 shorter events, 13.6 us)
Async XLA Ops:
  7.2 118.0 %copy-start.3 = (f32[640]{0:T(1024)S(1)}, f32[640]{0:T(1024)}, u32[]{:S(2)}) copy-start(f32[640]{0:T(1024)} %param.23) | copy-start | bytes 7684
  7.2 87.9 %all-gather.10.cloned.1.call-start = ((), (), s32[]{:S(2)}) async-start(), calls=%async_computation.2 | async-start | bytes 1392640 | tf_op jit(solution)/shard_map/all_gather | solution.py:112
  7.9 224.7 %all-gather.8.cloned.1.call-start = ((), (), s32[]{:S(2)}) async-start(), calls=%async_computation.1 | async-start | bytes 5570560 | tf_op jit(solution)/shard_map/all_gather | solution.py:99
  8.7 288.4 %all-gather.12.cloned.1.call-start = ((), (), s32[]{:S(2)}) async-start(), calls=%async_computation.3 | async-start | bytes 6553600 | tf_op jit(solution)/shard_map/all_gather | solution.py:116
  125.2 2.8 copy-start
  125.2 2.8 copy-start.4
  126.6 2.3 copy-start.7
  126.6 4.9 copy-start.8
  126.6 5.5 %copy-start.9 = (s32[4]{0:T(128)S(1)}, s32[4]{0:T(128)}, u32[]{:S(2)}) copy-start(s32[4]{0:T(128)} %param.19) | copy-start | bytes 52
  126.6 6.7 %copy-start.5 = (f32[640]{0:T(1024)S(1)}, f32[640]{0:T(1024)}, u32[]{:S(2)}) copy-start(f32[640]{0:T(1024)} %param.17) | copy-start | bytes 7684
  127.9 300.1 %all-gather.6.cloned.1.call-start = ((), (), s32[]{:S(2)}) async-start(), calls=%async_computation | async-start | bytes 5570560 | tf_op jit(solution)/shard_map/all_gather | solution.py:98
  297.0 1.9 copy-start.6
  451.2 1.1 copy-start.1
  454.4 0.9 copy-start.2
  458.8 1.1 copy-start.1
  462.0 0.9 copy-start.2
  466.4 1.1 copy-start.1
  469.7 0.9 copy-start.2
  474.0 1.1 copy-start.1
  477.3 0.9 copy-start.2
  481.6 1.1 copy-start.1
  484.9 0.9 copy-start.2
  489.2 1.1 copy-start.1
  492.5 0.9 copy-start.2
  496.8 1.1 copy-start.1
  500.1 0.9 copy-start.2
  504.4 1.1 copy-start.1
  507.7 0.9 copy-start.2
Sparse Core Ops, SparseCore 0:
  10.1 84.9 all-gather.9
  97.1 135.4 all-gather.7
  234.7 62.2 all-gather.11
  299.5 128.4 all-gather.5
where the time goes:
time: 520 us; the launch traced here: 517 us
  waiting for transfers between devices  353 us (68%)
  local copies, waits for them, and re-layouts  64.9 us (12%)
  matrix products  32.1 us (6%)
  blocking collectives  27.6 us (5%)
  other arithmetic  17.7 us (3%)
  between operations  16 us (3%)
  loops' own time  5.74 us (1%)
    all_gather x1, waiting for transfers between devices, per_device(): keys = lax.all_gather(k_hat[None], 'seq', axis=1, tiled=True)  126 us
    all_gather x1, waiting for transfers between devices, per_device(): values = lax.all_gather(v_self, 'seq', axis=1, tiled=True)  98.9 us
    all_gather x1, waiting for transfers between devices, per_device(): whole = lax.all_gather(cap_kv, 'seq', axis=2, tiled=True)  82.7 us
    all_gather x1, waiting for transfers between devices, per_device(): routed = lax.all_gather(assembled, 'section', axis=1, tiled=True)  44.5 us
    psum x1, blocking collectives, per_device(): lax.psum((square_sums(q_self[0]), square_sums(k_self[0]), square_sums(q_c...  27.6 us
    unnamed x23, local copies, waits for them, and re-layouts  18.7 us
    dot_general x9, matrix products, one_block(): jnp.einsum('hqk,khd->hqd', weights.astype(jnp.bfloat16), value_block, pre...  18 us
    dot_general x9, matrix products, one_block(): jnp.einsum('qhd,khd->hqk', queries, key_block, preferred_element_type=jnp...  14.2 us
  transfers between devices with their start and end apart: 4, of which 4 were waited for; matrix products, arithmetic and copies ran while one was open for 7% of the time, Pallas kernels for 0%

commit v1 on v0

--- a/solution.py
+++ b/solution.py
@@ -113,7 +113,30 @@
     key_totals = lax.psum(square_sums(whole[0, 0]), "wide")
     own_keys = scaled_rows(whole[0, 0], key_totals, gain_k_cross)
     assembled = jnp.stack([own_keys, whole[1, 0]])[:, None]
-    routed = lax.all_gather(assembled, "section", axis=1, tiled=True)
+    peers, place, width_2 = (
+        lax.axis_size("section"),
+        lax.axis_index("section"),
+        assembled.shape[1],
+    )
+    upward = [(i, (i + 1) % peers) for i in range(peers)]
+    left = [(i, (i - 1) % peers) for i in range(peers)]
+    whole_2 = jnp.zeros(
+        (*assembled.shape[:1], peers * width_2, *assembled.shape[1 + 1 :]), assembled.dtype
+    )
+    whole_2 = lax.dynamic_update_slice_in_dim(whole_2, assembled, place * width_2, axis=1)
+    from_left = from_right = assembled
+    halfway = peers // 2
+    for hop in range(1, halfway + 1):
+        from_left = lax.ppermute(from_left, "section", upward)
+        whole_2 = lax.dynamic_update_slice_in_dim(
+            whole_2, from_left, (place - hop) % peers * width_2, axis=1
+        )
+        if hop < peers - halfway:
+            from_right = lax.ppermute(from_right, "section", left)
+            whole_2 = lax.dynamic_update_slice_in_dim(
+                whole_2, from_right, (place + hop) % peers * width_2, axis=1
+            )
+    routed = whole_2
     chosen = lax.dynamic_index_in_dim(routed, source, 1, keepdims=False)
     count_rows = chosen.shape[1]
     cross_state = attend_rows(

time: 520 us -> 454 us (0.87)
  waiting for transfers between devices: 353 us -> 270 us
  local copies, waits for them, and re-layouts: 64.9 us -> 74.6 us
  starting transfers between devices: 0.16 us -> 9.02 us
    all_gather x1, waiting for transfers between devices: 98.9 us -> 29.5 us  [per_device(): values = lax.all_gather(v_self, 'seq', axis=1, tiled=True)]
    ppermute x0 -> x3, waiting for transfers between devices: none -> 48.2 us  [the longest x2 48.2 us: per_device(): from_left = lax.ppermute(from_left, 'section', upward)]
    all_gather x1 -> x0, waiting for transfers between devices: 44.5 us -> none  [per_device(): routed = lax.all_gather(assembled, 'section', axis=1, tiled=True)]
    all_gather x1, waiting for transfers between devices: 126 us -> 109 us  [per_device(): keys = lax.all_gather(k_hat[None], 'seq', axis=1, tiled=True)]
    ppermute x0 -> x3, starting transfers between devices: none -> 8.9 us  [the longest x2 5.5 us: per_device(): from_left = lax.ppermute(from_left, 'section', upward)]
    unnamed x23 -> x34, local copies, waits for them, and re-layouts: 18.7 us -> 22.7 us
  transfers between devices with their start and end apart: 4 -> 6, of which waited for: 4 -> 5; matrix products, arithmetic and copies ran while one was open for 7% -> 10% of each run, Pallas kernels for 0% -> 0%
where the time goes in v1:
time: 454 us; the launch traced here: 451 us
  waiting for transfers between devices  270 us (59%)
  local copies, waits for them, and re-layouts  74.6 us (16%)
  matrix products  32.2 us (7%)
  blocking collectives  27.8 us (6%)
  other arithmetic  16.2 us (4%)
  between operations  16.1 us (4%)
  starting transfers between devices  9.02 us (2%)
  loops' own time  5.74 us (1%)
    all_gather x1, waiting for transfers between devices, per_device(): keys = lax.all_gather(k_hat[None], 'seq', axis=1, tiled=True)  109 us
    all_gather x1, waiting for transfers between devices, per_device(): whole = lax.all_gather(cap_kv, 'seq', axis=2, tiled=True)  82.8 us
    ppermute x2, waiting for transfers between devices, per_device(): from_left = lax.ppermute(from_left, 'section', upward)  48.2 us
    all_gather x1, waiting for transfers between devices, per_device(): values = lax.all_gather(v_self, 'seq', axis=1, tiled=True)  29.5 us
    psum x1, blocking collectives, per_device(): lax.psum((square_sums(q_self[0]), square_sums(k_self[0]), square_sums(q_c...  27.8 us
    unnamed x34, local copies, waits for them, and re-layouts  22.7 us
    dot_general x9, matrix products, one_block(): jnp.einsum('hqk,khd->hqd', weights.astype(jnp.bfloat16), value_block, pre...  18 us
    dot_general x9, matrix products, one_block(): jnp.einsum('qhd,khd->hqk', queries, key_block, preferred_element_type=jnp...  14.2 us
  transfers between devices with their start and end apart: 6, of which 5 were waited for; matrix products, arithmetic and copies ran while one was open for 10% of the time, Pallas kernels for 0%

profile of v1, /device:TPU:1, one launch (start us, length us, event | category | flops | bytes accessed | tf_op | source)
XLA Modules:
  0.0 451.3 jit_solution(8302205823356561793)
XLA Ops:
  7.2 1.6 copy.45
  8.9 0.7 all-gather.6.cloned.1.call-update
  9.7 1.1 copy.44
  10.8 1.3 copy.38
  12.8 82.8 %all-gather.8.cloned.1.call-done = bf16[2,1,512,640]{3,0,1,2:T(2,128)(2,1)} async-done(((bf16[2,1,32,640]{3,0,1,2:T(2,128)(2,1)}), bf16[2,1,512,640]{3,0,1,2:T(2,128)(2,1)}) %all-gather.8.cloned.1.call-update) | async-done | bytes 1310736 | tf_op jit(solution)/shard_map/all_gather | solution.py:112
  95.6 4.0 fusion.56
  99.7 1.0 copy.59
  100.8 27.8 %all-reduce = (f32[256]{0:T(256)S(1)}, f32[256]{0:T(256)S(1)}, f32[512]{0:T(512)S(1)}, f32[256]{0:T(256)S(1)}) all-reduce(f32[256]{0:T(256)S(1)} %fusion.47, f32[256]{0:T(256)S(1)} %multiply_reduce_fusion.1, f32[512]{0:T(512)S(1)} %fusion.28, f32[256]{0:T(256)S(1)} %multiply_reduce_fusion), channel_id=1, replica_groups=mesh['section'=4,'seq'=16,'wide'=8] {'wide'}, use_global_device_ids=true, to_apply=%region_1.2 | all-reduce | flops 1280 | bytes 10240 | tf_op jit(solution)/shard_map/psum | solution.py:92
  128.6 1.8 fusion.49
  130.5 1.0 copy.60
  131.7 1.2 maximum_bitcast_fusion
  132.9 3.1 collective-permute-start
  136.0 3.4 collective-permute-start.1
  139.4 26.8 %collective-permute-done = bf16[2,1,512,640]{2,3,1,0:T(8,128)(2,1)} collective-permute-done((bf16[2,1,512,640]{2,3,1,0:T(8,128)(2,1)}, bf16[2,1,512,640]{2,3,1,0:T(8,128)(2,1)}, u32[]{:S(2)}, u32[]{:S(2)}) %collective-permute-start) | collective-permute-done | bytes 1310752 | tf_op jit(solution)/shard_map/ppermute | solution.py:130
  166.2 2.4 collective-permute-start.2
  168.7 0.6 fusion.53
  171.3 0.7 dynamic_slice.31
  172.5 0.7 iota_compare_fusion
  174.2 1.4 constant_dynamic-update-slice_fusion.2
  175.7 1.4 constant_dynamic-update-slice_fusion.1
  177.2 21.4 %collective-permute-done.2 = bf16[2,1,512,640]{2,3,1,0:T(8,128)(2,1)} collective-permute-done((bf16[2,1,512,640]{2,3,1,0:T(8,128)(2,1)}, bf16[2,1,512,640]{2,3,1,0:T(8,128)(2,1)}, u32[]{:S(2)}, u32[]{:S(2)}) %collective-permute-start.2) | collective-permute-done | bytes 1310752 | tf_op jit(solution)/shard_map/ppermute | solution.py:130
  198.6 1.4 constant_dynamic-update-slice_fusion
  200.1 1.0 fusion.22
  201.1 0.8 fusion.23
  201.9 0.8 fusion.44
  202.7 0.9 copy.51
  203.6 29.5 %all-gather.6.cloned.1.call-done = bf16[1,4096,640]{2,1,0:T(8,128)(2,1)} async-done(((bf16[1,256,640]{2,1,0:T(8,128)(2,1)}), bf16[1,4096,640]{2,1,0:T(8,128)(2,1)}) %all-gather.6.cloned.1.call-update) | async-done | bytes 5242896 | tf_op jit(solution)/shard_map/all_gather | solution.py:99
  233.1 12.7 %reshape.179 = bf16[8,512,5,128]{3,2,1,0:T(8,128)(2,1)} reshape(bf16[1,4096,640]{2,1,0:T(8,128)(2,1)} %all-gather.6.cloned.1.call-done) | data formatting | bytes 10485760 | tf_op jit(solution)/shard_map/reshape;reshape;squeeze | solution.py:36
  245.8 7.1 %copy.42 = bf16[8,512,5,128]{3,1,2,0:T(8,128)(2,1)} copy(bf16[8,512,5,128]{3,2,1,0:T(8,128)(2,1)} %reshape.179) | data formatting | bytes 10485760
  252.9 108.6 %all-gather.4.cloned.1.call-done = bf16[1,4096,640]{2,1,0:T(8,128)(2,1)} async-done(((bf16[1,256,640]{2,1,0:T(8,128)(2,1)}), bf16[1,4096,640]{2,1,0:T(8,128)(2,1)}) %all-gather.4.cloned.1.call-update) | async-done | bytes 5242896 | tf_op jit(solution)/shard_map/all_gather | solution.py:98
  361.5 12.7 %reshape.178 = bf16[8,512,5,128]{3,2,1,0:T(8,128)(2,1)} reshape(bf16[1,4096,640]{2,1,0:T(8,128)(2,1)} %all-gather.4.cloned.1.call-done) | data formatting | bytes 10485760 | tf_op jit(solution)/shard_map/reshape;reshape;squeeze | solution.py:35
  374.2 7.2 %copy.40 = bf16[8,512,5,128]{3,1,2,0:T(8,128)(2,1)} copy(bf16[8,512,5,128]{3,2,1,0:T(8,128)(2,1)} %reshape.178) | data formatting | bytes 10485760
  381.4 61.1 %while.3 = (s32[]{:T(128)}, f32[5,256]{1,0:T(8,128)S(1)}, f32[5,256]{1,0:T(8,128)S(1)}, f32[5,256,128]{2,1,0:T(8,128)}, s32[8]{0:T(128)S(1)}, /*index=5*/s32[]{:...) while((s32[]{:T(128)}, f32[5,256]{1,0:T(8,128)S(1)}, ...), condition=%wide.region_7.8_spmd.clone, body=%wide.region_4.7_spmd.clone.sunk | while | flops 343252224 | bytes 16141529 | solution.py:62
  382.6 0.6 add_compare_fusion.2
  383.3 1.7 bitcast_reduce_fusion.2
  386.0 2.1 fusion.72
  388.2 0.9 copy-done.6
  390.3 0.6 add_compare_fusion.2
  390.9 1.6 bitcast_reduce_fusion.2
  393.7 2.1 fusion.72
  395.8 0.9 copy-done.6
  397.9 0.6 add_compare_fusion.2
  398.6 1.6 bitcast_reduce_fusion.2
  401.3 2.1 fusion.72
  403.5 0.9 copy-done.6
  405.6 0.6 add_compare_fusion.2
  406.2 1.7 bitcast_reduce_fusion.2
  409.0 2.1 fusion.72
  411.1 0.9 copy-done.6
  413.8 1.6 bitcast_reduce_fusion.2
  416.6 2.1 fusion.72
  418.7 0.9 copy-done.6
  420.8 0.6 add_compare_fusion.2
  421.5 1.7 bitcast_reduce_fusion.2
  424.2 2.1 fusion.72
  426.4 0.9 copy-done.6
  429.1 1.6 bitcast_reduce_fusion.2
  431.9 2.1 fusion.72
  434.0 0.9 copy-done.6
  436.7 1.7 bitcast_reduce_fusion.2
  439.5 2.1 fusion.72
  441.7 0.9 copy-done.6
  442.5 1.3 copy.43
  443.9 0.9 copy.50
  (118 shorter events, 18.1 us)
Async XLA Ops:
  7.2 5.2 %copy-start.4 = (bf16[1,256,640]{2,1,0:T(8,128)(2,1)S(1)}, bf16[1,256,640]{2,1,0:T(8,128)(2,1)}, u32[]{:S(2)}) copy-start(bf16[1,256,640]{2,1,0:T(8,128)(2,1)} %param.15) | copy-start | bytes 983044
  7.2 88.4 %all-gather.8.cloned.1.call-start = ((), (), s32[]{:S(2)}) async-start(), calls=%async_computation.2 | async-start | bytes 1392640 | tf_op jit(solution)/shard_map/all_gather | solution.py:112
  8.9 224.2 %all-gather.6.cloned.1.call-start = ((), (), s32[]{:S(2)}) async-start(), calls=%async_computation.1 | async-start | bytes 5570560 | tf_op jit(solution)/shard_map/all_gather | solution.py:99
  9.6 351.9 %all-gather.4.cloned.1.call-start = ((), (), s32[]{:S(2)}) async-start(), calls=%async_computation | async-start | bytes 5570560 | tf_op jit(solution)/shard_map/all_gather | solution.py:98
  10.8 1.7 copy-start
  12.1 0.7 copy-start.2
  99.6 29.0 %copy-start.7 = (f32[640]{0:T(1024)S(1)}, f32[640]{0:T(1024)}, u32[]{:S(2)}) copy-start(f32[640]{0:T(1024)} %param.18) | copy-start | bytes 7684
  99.7 31.9 %copy-start.8 = (f32[640]{0:T(1024)S(1)}, f32[640]{0:T(1024)}, u32[]{:S(2)}) copy-start(f32[640]{0:T(1024)} %param.23) | copy-start | bytes 7684
  130.5 38.2 %copy-start.11 = (s32[4]{0:T(128)S(1)}, s32[4]{0:T(128)}, u32[]{:S(2)}) copy-start(s32[4]{0:T(128)} %param.25) | copy-start | bytes 52
  130.5 40.8 %copy-start.12 = (s32[4]{0:T(128)S(1)}, s32[4]{0:T(128)}, u32[]{:S(2)}) copy-start(s32[4]{0:T(128)} %param.24) | copy-start | bytes 52
  130.5 41.4 %copy-start.13 = (s32[4]{0:T(128)S(1)}, s32[4]{0:T(128)}, u32[]{:S(2)}) copy-start(s32[4]{0:T(128)} %param.19) | copy-start | bytes 52
  130.5 42.7 %copy-start.9 = (f32[640]{0:T(1024)S(1)}, f32[640]{0:T(1024)}, u32[]{:S(2)}) copy-start(f32[640]{0:T(1024)} %param.17) | copy-start | bytes 7684
  131.5 41.7 %copy-start.3 = (bf16[1,256,640]{1,2,0:T(8,128)(2,1)S(1)}, bf16[1,256,640]{1,2,0:T(8,128)(2,1)}, u32[]{:S(2)}) copy-start(bf16[1,256,640]{1,2,0:T(8,128)(2,1)} %copy-done.2) | copy-start | bytes 983044
  132.9 33.3 %collective-permute-start = (bf16[2,1,512,640]{2,3,1,0:T(8,128)(2,1)}, bf16[2,1,512,640]{2,3,1,0:T(8,128)(2,1)}, u32[]{:S(2)}, u32[]{:S(2)}) collective-permute-start(bf16[2,1,512,640]{2,3,1,0:T(8,128)(2,1)} %maximum_bitcast_fusion), channel_id=1, source_target_pairs={{0,128},{128,256},{256,384},{384,0},{1,129},{129,257},{257,385},{3... | collective-permute-start | bytes 3932168 | tf_op jit(solution)/shard_map/ppermute | solution.py:130
  136.0 39.7 %collective-permute-start.1 = (bf16[2,1,512,640]{2,3,1,0:T(8,128)(2,1)}, bf16[2,1,512,640]{2,3,1,0:T(8,128)(2,1)}, u32[]{:S(2)}, u32[]{:S(2)}) collective-permute-start(bf16[2,1,512,640]{2,3,1,0:T(8,128)(2,1)} %maximum_bitcast_fusion), channel_id=1, source_target_pairs={{0,384},{128,0},{256,128},{384,256},{1,385},{129,1},{257,129},{385... | collective-permute-start | bytes 3932168 | tf_op jit(solution)/shard_map/ppermute | solution.py:135
  166.2 32.4 %collective-permute-start.2 = (bf16[2,1,512,640]{2,3,1,0:T(8,128)(2,1)}, bf16[2,1,512,640]{2,3,1,0:T(8,128)(2,1)}, u32[]{:S(2)}, u32[]{:S(2)}) collective-permute-start(bf16[2,1,512,640]{2,3,1,0:T(8,128)(2,1)} %collective-permute-done), channel_id=1, source_target_pairs={{0,128},{128,256},{256,384},{384,0},{1,129},{129,257},{257,385},{3... | collective-permute-start | bytes 3932168 | tf_op jit(solution)/shard_map/ppermute | solution.py:130
  177.1 23.0 %copy-start.1 = (bf16[1,256,640]{1,2,0:T(8,128)(2,1)S(1)}, bf16[1,256,640]{1,2,0:T(8,128)(2,1)}, u32[]{:S(2)}) copy-start(bf16[1,256,640]{1,2,0:T(8,128)(2,1)} %copy-done) | copy-start | bytes 983044
  177.1 23.0 %copy-start.10 = (f32[640]{0:T(1024)S(1)}, f32[640]{0:T(1024)}, u32[]{:S(2)}) copy-start(f32[640]{0:T(1024)} %param.22) | copy-start | bytes 7684
  384.9 1.1 copy-start.5
  388.2 0.9 copy-start.6
  392.6 1.1 copy-start.5
  395.8 0.9 copy-start.6
  400.2 1.1 copy-start.5
  403.5 0.9 copy-start.6
  407.9 1.1 copy-start.5
  411.1 0.9 copy-start.6
  415.5 1.1 copy-start.5
  418.7 0.9 copy-start.6
  423.1 1.1 copy-start.5
  426.4 0.9 copy-start.6
  430.8 1.1 copy-start.5
  434.0 0.9 copy-start.6
  438.4 1.1 copy-start.5
  441.7 0.9 copy-start.6
Sparse Core Ops, SparseCore 0:
  10.7 84.8 all-gather.7
  97.7 135.3 all-gather.5
  235.8 125.7 all-gather.3
